TPU v7x, 32 devices: a whole 2x2x4 slice. The times are simulated.
32 devices in a mesh: ctx: 8 (over z, x), fsdp: 4 (over y, core).
Axes of the slice: x: 2, y: 2, z: 4, core: 2. Of those that a mesh axis runs over, the one named last changes fastest.
Arguments:
- inputs: bfloat16 [2, 4, 4096, 512], P(None, 'fsdp', 'ctx'), may hold values from -6 to 6
- out_grad: bfloat16 [2, 4, 4096, 512], P(None, 'fsdp', 'ctx'), may hold values from -6 to 6
- segment_ids: int32 [2, 4, 4096], P(None, 'fsdp', 'ctx'), may hold values from 0 to 15, never falling along the last dimension, each value on 1 to 2048 neighbouring positions
- block_order: int32 [16], replicated, may hold values from 0 to 15, each once
- w_qkv: bfloat16 [512, 1536], P('fsdp'), may hold values from -0.25 to 0.25
- w_out: bfloat16 [512, 512], P('fsdp'), may hold values from -1 to 1
- w_up: bfloat16 [512, 2048], P('fsdp'), may hold values from -0.25 to 0.25
- w_down: bfloat16 [2048, 512], P('fsdp'), may hold values from -0.125 to 0.125
- norm1_gain: bfloat16 [512], P('fsdp'), may hold values from 0.25 to 1.75
- norm1_bias: bfloat16 [512], P('fsdp'), may hold values from -2 to 2
- norm2_gain: bfloat16 [512], P('fsdp'), may hold values from 0.25 to 1.75
- norm2_bias: bfloat16 [512], P('fsdp'), may hold values from -2 to 2
- out_bias: bfloat16 [512], P('fsdp'), may hold values from -2 to 2
- up_bias: bfloat16 [2048], P('fsdp'), may hold values from -3 to 3
- down_bias: bfloat16 [512], P('fsdp'), may hold values from -2 to 2
Outputs:
- outputs: bfloat16 [2, 4, 4096, 512], P(None, 'fsdp', 'ctx')
- input_grad: float32 [2, 4, 4096, 512], P(None, 'fsdp', 'ctx')
- grad_w_qkv: float32 [512, 1536], P('fsdp')
- grad_w_out: float32 [512, 512], P('fsdp')
- grad_w_up: float32 [512, 2048], P('fsdp')
- grad_w_down: float32 [2048, 512], P('fsdp')
- grad_norm1_gain: float32 [512], P('fsdp')
- grad_norm1_bias: float32 [512], P('fsdp')
- grad_norm2_gain: float32 [512], P('fsdp')
- grad_norm2_bias: float32 [512], P('fsdp')
- grad_out_bias: float32 [512], P('fsdp')
- grad_up_bias: float32 [2048], P('fsdp')
- grad_down_bias: float32 [512], P('fsdp')
Inputs may be any that keep to these rules, and one draw needn't show every extreme that they name: `segment_ids`: along each sequence's true positions document numbers start at 0 and never fall; each document has 1 to 2048 tokens and one has exactly 2048. `block_order`: each value appears exactly once.
All inputs are finite; a program needn't handle non-finite values.
Results may differ from a plain program's by a relative error of at most 0.02.
Values may be sent and summed in bfloat16 or wider, within the bound.
A program may use at most 256 MiB of HBM per device.

v0:
```python
import math
import jax
import jax.numpy as jnp
from jax import lax
from jax.sharding import PartitionSpec as P

H = 8
HD = 64
BLK = 256
norm_eps = 1e-05
mask_fill = -1e30


def layer_norm(values, gain_vec, offset):
    center = values - jnp.mean(values, axis=-1, keepdims=True)
    spread = jnp.mean(center * center, axis=-1, keepdims=True)
    return center * lax.rsqrt(spread + norm_eps) * gain_vec + offset


def gelu_exact(values):
    return 0.5 * values * (1.0 + lax.erf(values * (1.0 / math.sqrt(2.0))))


def score_block(query_heads, key_heads, query_doc, query_pos, key_doc, key_pos):
    raw_scores = jnp.einsum(
        "qhd,khd->hqk", query_heads, key_heads, preferred_element_type=jnp.float32
    ) * (1.0 / math.sqrt(HD))
    allowed = (query_doc[:, None] == key_doc[None, :]) & (key_pos[None, :] <= query_pos[:, None])
    return (raw_scores, allowed[None])


def soft_block(raw_scores, allowed, log_norm):
    return jnp.exp(jnp.where(allowed, raw_scores, mask_fill) - log_norm[:, :, None])


def row_log_norm(query_heads, key_blocks, doc_blocks, pos_blocks, query_doc, query_pos):

    def row_visit(running, block_item):
        row_top, row_sum = running
        key_heads, key_doc, key_pos = block_item
        raw_scores, allowed = score_block(
            query_heads, key_heads, query_doc, query_pos, key_doc, key_pos
        )
        masked = jnp.where(allowed, raw_scores, mask_fill)
        new_top = jnp.maximum(row_top, jnp.max(masked, axis=-1))
        fresh = jnp.sum(jnp.where(allowed, jnp.exp(masked - new_top[:, :, None]), 0.0), axis=-1)
        return ((new_top, row_sum * jnp.exp(row_top - new_top) + fresh), None)

    query_count = query_doc.shape[0]
    start = (
        jnp.full((H, query_count), mask_fill, jnp.float32),
        jnp.zeros((H, query_count), jnp.float32),
    )
    (row_top, row_sum), unused = lax.scan(row_visit, start, (key_blocks, doc_blocks, pos_blocks))
    return row_top + jnp.log(row_sum)


def attend(
    query_heads, key_blocks, value_blocks, doc_blocks, pos_blocks, query_doc, query_pos, log_norm
):

    def attend_visit(accum_out, block_item):
        key_heads, value_heads, key_doc, key_pos = block_item
        raw_scores, allowed = score_block(
            query_heads, key_heads, query_doc, query_pos, key_doc, key_pos
        )
        soft_low = soft_block(raw_scores, allowed, log_norm).astype(jnp.bfloat16)
        return (
            accum_out
            + jnp.einsum("hqk,khd->qhd", soft_low, value_heads, preferred_element_type=jnp.float32),
            None,
        )

    start = jnp.zeros(query_heads.shape, jnp.float32)
    accum_out, unused = lax.scan(
        attend_visit, start, (key_blocks, value_blocks, doc_blocks, pos_blocks)
    )
    return accum_out


def grad_block(
    query_heads,
    grad_heads,
    log_norm,
    row_delta,
    query_doc,
    query_pos,
    key_heads,
    value_heads,
    key_doc,
    key_pos,
):
    raw_scores, allowed = score_block(
        query_heads, key_heads, query_doc, query_pos, key_doc, key_pos
    )
    soft = soft_block(raw_scores, allowed, log_norm)
    grad_soft = jnp.einsum(
        "qhd,khd->hqk", grad_heads, value_heads, preferred_element_type=jnp.float32
    )
    grad_scores = (soft * (grad_soft - row_delta[:, :, None])).astype(jnp.bfloat16)
    score_scale = 1.0 / math.sqrt(HD)
    part_q = (
        jnp.einsum("hqk,khd->qhd", grad_scores, key_heads, preferred_element_type=jnp.float32)
        * score_scale
    )
    part_k = (
        jnp.einsum("hqk,qhd->khd", grad_scores, query_heads, preferred_element_type=jnp.float32)
        * score_scale
    )
    part_v = jnp.einsum(
        "hqk,qhd->khd", soft.astype(jnp.bfloat16), grad_heads, preferred_element_type=jnp.float32
    )
    return (part_q, part_k, part_v)


def body(
    inputs,
    out_grad,
    segment_ids,
    block_order,
    w_qkv,
    w_out,
    w_up,
    w_down,
    norm1_gain,
    norm1_bias,
    norm2_gain,
    norm2_bias,
    out_bias,
    up_bias,
    down_bias,
):
    gathered = (
        lax.all_gather(w_qkv, "fsdp", axis=0, tiled=True),
        lax.all_gather(w_out, "fsdp", axis=0, tiled=True),
        lax.all_gather(w_up, "fsdp", axis=0, tiled=True),
        lax.all_gather(w_down, "fsdp", axis=0, tiled=True),
        lax.all_gather(norm1_gain, "fsdp", axis=0, tiled=True),
        lax.all_gather(norm1_bias, "fsdp", axis=0, tiled=True),
        lax.all_gather(norm2_gain, "fsdp", axis=0, tiled=True),
        lax.all_gather(norm2_bias, "fsdp", axis=0, tiled=True),
        lax.all_gather(out_bias, "fsdp", axis=0, tiled=True),
        lax.all_gather(up_bias, "fsdp", axis=0, tiled=True),
        lax.all_gather(down_bias, "fsdp", axis=0, tiled=True),
    )
    full_qkv, full_out, full_up, full_down = (gathered[0], gathered[1], gathered[2], gathered[3])
    gain_one, bias_one, gain_two, bias_two, full_obias, full_ubias, full_dbias = [
        member.astype(jnp.float32) for member in gathered[4:]
    ]
    model_width = full_qkv.shape[0]
    local_rows = inputs.shape[2]
    ctx_count = lax.axis_size("ctx")
    seq_len = local_rows * ctx_count
    key_block = min(512, seq_len)
    block_count = seq_len // key_block
    ctx_index = lax.axis_index("ctx")
    row_ids = jnp.arange(local_rows, dtype=jnp.int32)
    own_blocks = lax.dynamic_slice_in_dim(block_order, 2 * ctx_index, 2)
    own_pos = own_blocks[row_ids // BLK] * BLK + row_ids % BLK
    all_ids = jnp.arange(seq_len, dtype=jnp.int32)
    all_pos = block_order[all_ids // BLK] * BLK + all_ids % BLK
    pos_blocks = all_pos.reshape(block_count, key_block)
    grad_sums = [jnp.zeros(member.shape, jnp.float32) for member in gathered]
    outputs_list = []
    input_grads = []
    for micro_idx in range(inputs.shape[0]):
        seq_in = inputs[micro_idx, 0].astype(jnp.float32)
        normed, norm1_pull = jax.vjp(layer_norm, seq_in, gain_one, bias_one)
        normed_low = normed.astype(jnp.bfloat16)
        qkv_out = jnp.dot(normed_low, full_qkv, preferred_element_type=jnp.float32).astype(
            jnp.bfloat16
        )
        query_heads = qkv_out[:, :model_width].reshape(local_rows, H, HD)
        kv_all, doc_all = (
            lax.all_gather(qkv_out[:, model_width:], "ctx", axis=0, tiled=True),
            lax.all_gather(segment_ids[micro_idx, 0], "ctx", axis=0, tiled=True),
        )
        doc_rows = doc_all[all_pos]
        query_doc = doc_all[own_pos]
        kv_heads = kv_all.reshape(block_count, key_block, 2, H, HD)
        key_blocks = kv_heads[:, :, 0]
        value_blocks = kv_heads[:, :, 1]
        doc_blocks = doc_rows.reshape(block_count, key_block)
        log_norm = row_log_norm(query_heads, key_blocks, doc_blocks, pos_blocks, query_doc, own_pos)
        attn_acc = attend(
            query_heads,
            key_blocks,
            value_blocks,
            doc_blocks,
            pos_blocks,
            query_doc,
            own_pos,
            log_norm,
        )
        attn_low = attn_acc.reshape(local_rows, model_width).astype(jnp.bfloat16)
        branch = jnp.dot(attn_low, full_out, preferred_element_type=jnp.float32) + full_obias
        middle = seq_in + branch
        normed_two, norm2_pull = jax.vjp(layer_norm, middle, gain_two, bias_two)
        normed_two_low = normed_two.astype(jnp.bfloat16)
        hidden = jnp.dot(normed_two_low, full_up, preferred_element_type=jnp.float32) + full_ubias
        active, gelu_pull = jax.vjp(gelu_exact, hidden)
        active_low = active.astype(jnp.bfloat16)
        result = middle + (
            jnp.dot(active_low, full_down, preferred_element_type=jnp.float32) + full_dbias
        )
        outputs_list.append(result.astype(jnp.bfloat16))
        grad_y = out_grad[micro_idx, 0]
        grad_y32 = grad_y.astype(jnp.float32)
        grad_sums[3] = grad_sums[3] + jnp.einsum(
            "rf,rd->fd", active_low, grad_y, preferred_element_type=jnp.float32
        )
        grad_sums[10] = grad_sums[10] + jnp.sum(grad_y32, axis=0)
        grad_active = jnp.einsum("rd,fd->rf", grad_y, full_down, preferred_element_type=jnp.float32)
        (grad_hidden,) = gelu_pull(grad_active)
        grad_hidden_low = grad_hidden.astype(jnp.bfloat16)
        grad_sums[2] = grad_sums[2] + jnp.einsum(
            "rd,rf->df", normed_two_low, grad_hidden_low, preferred_element_type=jnp.float32
        )
        grad_sums[9] = grad_sums[9] + jnp.sum(grad_hidden_low.astype(jnp.float32), axis=0)
        grad_normed_two = jnp.einsum(
            "rf,df->rd", grad_hidden_low, full_up, preferred_element_type=jnp.float32
        )
        grad_mid_ln, grad_gain_two, grad_bias_two = norm2_pull(grad_normed_two)
        grad_sums[6] = grad_sums[6] + grad_gain_two
        grad_sums[7] = grad_sums[7] + grad_bias_two
        grad_mid = grad_y32 + grad_mid_ln
        grad_mid_low = grad_mid.astype(jnp.bfloat16)
        grad_sums[1] = grad_sums[1] + jnp.einsum(
            "rd,re->de", attn_low, grad_mid_low, preferred_element_type=jnp.float32
        )
        grad_sums[8] = grad_sums[8] + jnp.sum(grad_mid_low.astype(jnp.float32), axis=0)
        grad_attn_low = jnp.einsum(
            "re,de->rd", grad_mid_low, full_out, preferred_element_type=jnp.float32
        ).astype(jnp.bfloat16)
        grad_heads = grad_attn_low.reshape(local_rows, H, HD)
        row_delta = jnp.sum(grad_heads.astype(jnp.float32) * attn_acc, axis=-1).T

        def back_visit(grad_query, block_item):
            key_heads, value_heads, key_doc, key_pos = block_item
            part_q, part_k, part_v = grad_block(
                query_heads,
                grad_heads,
                log_norm,
                row_delta,
                query_doc,
                own_pos,
                key_heads,
                value_heads,
                key_doc,
                key_pos,
            )
            joined = jnp.concatenate(
                [part_k.reshape(key_block, model_width), part_v.reshape(key_block, model_width)],
                axis=1,
            )
            return (grad_query + part_q, joined)

        grad_query, kv_terms = lax.scan(
            back_visit,
            jnp.zeros((local_rows, H, HD), jnp.float32),
            (key_blocks, value_blocks, doc_blocks, pos_blocks),
        )
        kv_grad = lax.psum_scatter(
            kv_terms.reshape(seq_len, 2 * model_width).astype(jnp.bfloat16),
            "ctx",
            scatter_dimension=0,
            tiled=True,
        ).astype(jnp.float32)
        grad_qkv_low = jnp.concatenate(
            [grad_query.reshape(local_rows, model_width), kv_grad], axis=1
        ).astype(jnp.bfloat16)
        grad_sums[0] = grad_sums[0] + jnp.einsum(
            "rd,re->de", normed_low, grad_qkv_low, preferred_element_type=jnp.float32
        )
        grad_normed = jnp.einsum(
            "re,de->rd", grad_qkv_low, full_qkv, preferred_element_type=jnp.float32
        )
        grad_in_ln, grad_gain_one, grad_bias_one = norm1_pull(grad_normed)
        grad_sums[4] = grad_sums[4] + grad_gain_one
        grad_sums[5] = grad_sums[5] + grad_bias_one
        input_grads.append(grad_mid + grad_in_ln)
    owned = (
        lax.psum_scatter(
            grad_sums[0].astype(jnp.bfloat16), "fsdp", scatter_dimension=0, tiled=True
        ).astype(jnp.float32),
        lax.psum_scatter(
            grad_sums[1].astype(jnp.bfloat16), "fsdp", scatter_dimension=0, tiled=True
        ).astype(jnp.float32),
        lax.psum_scatter(
            grad_sums[2].astype(jnp.bfloat16), "fsdp", scatter_dimension=0, tiled=True
        ).astype(jnp.float32),
        lax.psum_scatter(
            grad_sums[3].astype(jnp.bfloat16), "fsdp", scatter_dimension=0, tiled=True
        ).astype(jnp.float32),
        lax.psum_scatter(
            grad_sums[4].astype(jnp.bfloat16), "fsdp", scatter_dimension=0, tiled=True
        ).astype(jnp.float32),
        lax.psum_scatter(
            grad_sums[5].astype(jnp.bfloat16), "fsdp", scatter_dimension=0, tiled=True
        ).astype(jnp.float32),
        lax.psum_scatter(
            grad_sums[6].astype(jnp.bfloat16), "fsdp", scatter_dimension=0, tiled=True
        ).astype(jnp.float32),
        lax.psum_scatter(
            grad_sums[7].astype(jnp.bfloat16), "fsdp", scatter_dimension=0, tiled=True
        ).astype(jnp.float32),
        lax.psum_scatter(
            grad_sums[8].astype(jnp.bfloat16), "fsdp", scatter_dimension=0, tiled=True
        ).astype(jnp.float32),
        lax.psum_scatter(
            grad_sums[9].astype(jnp.bfloat16), "fsdp", scatter_dimension=0, tiled=True
        ).astype(jnp.float32),
        lax.psum_scatter(
            grad_sums[10].astype(jnp.bfloat16), "fsdp", scatter_dimension=0, tiled=True
        ).astype(jnp.float32),
    )
    summed = (
        lax.psum(owned[0].astype(jnp.bfloat16), "ctx").astype(jnp.float32),
        lax.psum(owned[1].astype(jnp.bfloat16), "ctx").astype(jnp.float32),
        lax.psum(owned[2].astype(jnp.bfloat16), "ctx").astype(jnp.float32),
        lax.psum(owned[3].astype(jnp.bfloat16), "ctx").astype(jnp.float32),
        lax.psum(owned[4].astype(jnp.bfloat16), "ctx").astype(jnp.float32),
        lax.psum(owned[5].astype(jnp.bfloat16), "ctx").astype(jnp.float32),
        lax.psum(owned[6].astype(jnp.bfloat16), "ctx").astype(jnp.float32),
        lax.psum(owned[7].astype(jnp.bfloat16), "ctx").astype(jnp.float32),
        lax.psum(owned[8].astype(jnp.bfloat16), "ctx").astype(jnp.float32),
        lax.psum(owned[9].astype(jnp.bfloat16), "ctx").astype(jnp.float32),
        lax.psum(owned[10].astype(jnp.bfloat16), "ctx").astype(jnp.float32),
    )
    return (
        jnp.stack(outputs_list)[:, None],
        jnp.stack(input_grads)[:, None],
        summed[0],
        summed[1],
        summed[2],
        summed[3],
        summed[4],
        summed[5],
        summed[6],
        summed[7],
        summed[8],
        summed[9],
        summed[10],
    )


def solution(mesh):
    return jax.shard_map(
        body,
        mesh=mesh,
        in_specs=(
            P(None, "fsdp", "ctx", None),
            P(None, "fsdp", "ctx", None),
            P(None, "fsdp", "ctx"),
            P(),
            P("fsdp", None),
            P("fsdp", None),
            P("fsdp", None),
            P("fsdp", None),
            P("fsdp"),
            P("fsdp"),
            P("fsdp"),
            P("fsdp"),
            P("fsdp"),
            P("fsdp"),
            P("fsdp"),
        ),
        out_specs=(
            P(None, "fsdp", "ctx", None),
            P(None, "fsdp", "ctx", None),
            P("fsdp", None),
            P("fsdp", None),
            P("fsdp", None),
            P("fsdp", None),
            P("fsdp"),
            P("fsdp"),
            P("fsdp"),
            P("fsdp"),
            P("fsdp"),
            P("fsdp"),
            P("fsdp"),
        ),
        check_vma=False,
    )
```

profile of v0, /device:TPU:0, one launch (start us, length us, event | category | flops | bytes accessed | tf_op | source)
XLA Modules:
  0.0 1195.3 jit_solution(4293471570105327463)
XLA Ops:
  8.0 6.2 all-gather.2
  14.1 5.4 all-gather.3
  21.4 10.5 all-gather.15.cloned.1.call-done
  45.4 27.0 %all-gather = s32[1,1,4096]{2,1,0:T(1,128)S(1)} all-gather(s32[1,1,512]{2,1,0:T(1,128)S(1)} %get-tuple-element.1148), channel_id=2, replica_groups=mesh['ctx'=8,'fsdp'=4] {'ctx'}, dimensions={2}, use_global_device_ids=true | all-gather | bytes 18432 | tf_op jit(solution)/shard_map/all_gather | solution.py:176
  72.4 4.4 compare_select_fusion.14
  76.7 5.7 select_multiply_fusion.2
  85.7 23.0 %gather_fusion.1 = s32[4096]{0:T(1024)S(1)} fusion(s32[4096]{0:T(1024)S(1)} %bitcast.527, s32[4096]{0:T(1024)S(1)} %broadcast_clamp_fusion), kind=kCustom, calls=%fused_computation.1 | custom fusion | bytes 49152 | tf_op jit(solution)/shard_map/gather | solution.py:178
  108.7 26.7 %all-gather.1 = s32[1,1,4096]{2,1,0:T(1,128)S(1)} all-gather(s32[1,1,512]{2,1,0:T(1,128)S(1)} %get-tuple-element.1149), channel_id=3, replica_groups=mesh['ctx'=8,'fsdp'=4] {'ctx'}, dimensions={2}, use_global_device_ids=true | all-gather | bytes 18432 | tf_op jit(solution)/shard_map/all_gather | solution.py:176
  138.6 23.0 %gather_fusion.3 = s32[4096]{0:T(1024)S(1)} fusion(s32[4096]{0:T(1024)S(1)} %bitcast.529, s32[4096]{0:T(1024)S(1)} %broadcast_clamp_fusion), kind=kCustom, calls=%fused_computation.3 | custom fusion | bytes 49152 | tf_op jit(solution)/shard_map/gather | solution.py:178
  161.8 5.2 all-gather.5
  167.0 5.0 all-gather.6
  172.0 5.0 all-gather.4
  177.1 5.2 all-gather.7
  182.3 7.2 all_gather.50
  195.1 11.4 copy.162
  206.6 12.2 %copy.239 = bf16[128,8,8,512]{3,2,1,0:T(8,128)(2,1)} copy(bf16[128,8,8,512]{3,1,2,0:T(8,128)(2,1)} %bitcast.538) | data formatting | bytes 16777216
  218.8 5.3 slice_bitcast_fusion
  227.5 50.1 %while.76 = (s32[]{:T(128)}, f32[8,512]{1,0:T(8,128)S(1)}, f32[8,512]{1,0:T(8,128)S(1)}, s32[512]{0:T(512)S(1)}, s32[8,512]{1,0:T(8,128)S(1)}, /*index=5*/s32[8,...) while((s32[]{:T(128)}, f32[8,512]{1,0:T(8,128)S(1)}, ...), condition=%wide.region_15.16_spmd.clone, body=%wide.region_12.15_spmd.clone.sunk | while | flops 286030336 | bytes 18847896 | solution.py:54
  277.6 10.2 all-gather.17.cloned.1.call-done
  287.8 11.7 copy.155
  299.6 12.2 %copy.238 = bf16[128,8,8,512]{3,2,1,0:T(8,128)(2,1)} copy(bf16[128,8,8,512]{3,1,2,0:T(8,128)(2,1)} %bitcast.539) | data formatting | bytes 16777216
  311.8 5.3 slice_bitcast_fusion.2
  320.5 50.5 %while.74 = (s32[]{:T(128)}, f32[8,512]{1,0:T(8,128)S(1)}, f32[8,512]{1,0:T(8,128)S(1)}, s32[512]{0:T(512)S(1)}, s32[8,512]{1,0:T(8,128)S(1)}, /*index=5*/s32[8,...) while((s32[]{:T(128)}, f32[8,512]{1,0:T(8,128)S(1)}, ...), condition=%wide.region_5.6_spmd.clone, body=%wide.region_2.5_spmd.clone.sunk | while | flops 286030336 | bytes 18847896 | solution.py:54
  371.0 5.7 copy.158
  377.3 46.4 %while.75 = (s32[]{:T(128)}, f32[512,8,64]{0,2,1:T(8,128)S(1)}, bf16[8,512,8,64]{1,3,2,0:T(8,128)(2,1)}, s32[512]{0:T(512)S(1)}, s32[8,512]{1,0:T(8,128)S(1)}, /...) while((s32[]{:T(128)}, f32[512,8,64]{0,2,1:T(8,128)S(1)}, ...), condition=%wide.region_7.8_spmd.clone, body=%wide.region_6.7_spmd.clone.sunk | while | flops 546580992 | bytes 4234906 | solution.py:75
  378.9 4.2 fusion.351
  384.7 4.2 fusion.351
  424.7 5.7 copy.165
  430.4 46.4 %while.77 = (s32[]{:T(128)}, f32[512,8,64]{0,2,1:T(8,128)S(1)}, bf16[8,512,8,64]{1,3,2,0:T(8,128)(2,1)}, s32[512]{0:T(512)S(1)}, s32[8,512]{1,0:T(8,128)S(1)}, /...) while((s32[]{:T(128)}, f32[512,8,64]{0,2,1:T(8,128)S(1)}, ...), condition=%wide.region_17.18_spmd.clone, body=%wide.region_16.17_spmd.clone.sunk | while | flops 546580992 | bytes 4234906 | solution.py:75
  481.3 5.1 fusion.219
  486.4 5.9 convert_reduce_fusion
  497.7 6.1 multiply_convert_fusion.1
  521.1 4.3 broadcast.709.clone2
  525.5 138.9 %while.78 = (s32[]{:T(128)}, f32[512,8,64]{0,2,1:T(8,128)}, bf16[8,512,1024]{2,1,0:T(8,128)(2,1)}, bf16[8,512,8,64]{1,3,2,0:T(8,128)(2,1)}, s32[512]{0:T(512)S(1...) while((s32[]{:T(128)}, f32[512,8,64]{0,2,1:T(8,128)}, ...), condition=%wide.region_24.25_spmd.clone, body=%wide.region_23.24_spmd.clone.sunk | while | flops 1367353856 | bytes 51714240 | solution.py:258
  664.4 4.3 broadcast.709.clone2.1
  668.7 131.5 %while.79 = (s32[]{:T(128)}, f32[512,8,64]{0,2,1:T(8,128)}, bf16[8,512,1024]{2,1,0:T(8,128)(2,1)}, bf16[8,512,8,64]{1,3,2,0:T(8,128)(2,1)}, s32[512]{0:T(512)S(1...) while((s32[]{:T(128)}, f32[512,8,64]{0,2,1:T(8,128)}, ...), condition=%wide.region_32.33_spmd.clone, body=%wide.region_31.32_spmd.clone.sunk | while | flops 1367353856 | bytes 51714240 | solution.py:258
  773.3 4.2 fusion.393
  817.0 5.2 all-gather.8
  826.2 4.4 fusion.163
  830.6 4.2 fusion.179
  834.8 129.0 %reduce-scatter.9.cloned.1.call-done = bf16[512,1024]{1,0:T(8,128)(2,1)} async-done(((bf16[4096,1024]{1,0:T(8,128)(2,1)}), bf16[512,1024]{1,0:T(8,128)(2,1)}) %reduce-scatter.9.cloned.1.call-update) | async-done | bytes 1048592 | tf_op jit(solution)/shard_map/reduce_scatter | solution.py:263
  963.8 4.4 fusion.144
  987.0 34.2 %reduce-scatter.15.cloned.1.call-done = bf16[128,2048]{1,0:T(8,128)(2,1)} async-done(((bf16[512,2048]{1,0:T(8,128)(2,1)}), bf16[128,2048]{1,0:T(8,128)(2,1)}) %reduce-scatter.15.cloned.1.call-update) | async-done | bytes 524304 | tf_op jit(solution)/shard_map/reduce_scatter | solution.py:289
  1021.1 33.9 %reduce-scatter.17.cloned.1.call-done = bf16[512,512]{1,0:T(8,128)(2,1)} async-done(((bf16[2048,512]{1,0:T(8,128)(2,1)}), bf16[512,512]{1,0:T(8,128)(2,1)}) %reduce-scatter.17.cloned.1.call-update) | async-done | bytes 524304 | tf_op jit(solution)/shard_map/reduce_scatter | solution.py:292
  1055.0 31.5 %reduce-scatter.11.cloned.1.call-done = bf16[128,1536]{1,0:T(8,128)(2,1)} async-done(((bf16[512,1536]{1,0:T(8,128)(2,1)}), bf16[128,1536]{1,0:T(8,128)(2,1)}) %reduce-scatter.11.cloned.1.call-update) | async-done | bytes 393232 | tf_op jit(solution)/shard_map/reduce_scatter | solution.py:283
  1091.7 10.5 all-reduce.9
  1102.8 22.1 %all-reduce.7 = (bf16[128]{0:T(256)(128)(2,1)S(1)}, bf16[128]{0:T(256)(128)(2,1)S(1)}, bf16[128]{0:T(256)(128)(2,1)S(1)}, bf16[128]{0:T(256)(128)(2,1)S(1)}, bf1...) all-reduce(bf16[128]{0:T(256)(128)(2,1)S(1)} %dynamic-slice.1, ...), channel_id=1, replica_groups=mesh['ctx'=8,'fsdp'=4] {'ctx'}, use_global_device_ids=true, to_apply=%region_47.48 | all-reduce | flops 1280 | bytes 5120 | tf_op jit(solution)/shard_map/psum | solution.py:322
  1131.7 48.7 %all-reduce.12.cloned.1.call-done = (bf16[128,1536]{1,0:T(8,128)(2,1)}, bf16[128,512]{1,0:T(8,128)(2,1)}, bf16[128,2048]{1,0:T(8,128)(2,1)}, bf16[512,512]{1,0:T(8,128)(2,1)}) async-done(((bf16[128,1536]{1,0:T(8,128)(2,1)}, bf16[128,512]{1,0:T(8,128)(2,1)}, bf16[128,2048]{1,0:T(8,128)(2,1)}, bf16[512,512]{1,0:T(8,128)(2,1)}), (bf16[128,1536]{1,0:T(8,128)(2,1)}, bf16[128,512]{1,0:T(8,128)(2,1)}, ...) | async-done | bytes 1572880 | tf_op jit(solution)/shard_map/psum | solution.py:318
  (783 shorter events, 568.7 us)
Async XLA Ops:
  7.2 24.8 %all-gather.15.cloned.1.call-start = ((), (), s32[]{:S(2)}) async-start(), calls=%async_computation.6 | async-start | bytes 1966080 | tf_op jit(solution)/shard_map/all_gather | solution.py:134
  7.9 187.2 %all-gather.23.cloned.1.call-start = ((), (), s32[]{:S(2)}) async-start(), calls=%async_computation.10 | async-start | bytes 9437184 | tf_op jit(solution)/shard_map/all_gather | solution.py:175
  14.1 23.3 %copy-start.59 = (f32[4,1,128]{2,1,0:T(1,128)}, f32[4,1,128]{2,1,0:T(1,128)S(1)}, u32[]{:S(2)}) copy-start(f32[4,1,128]{2,1,0:T(1,128)S(1)} %convert_element_type.304) | copy-start | bytes 6148
  19.5 17.9 %copy-start.87 = (f32[4,1,128]{2,1,0:T(1,128)}, f32[4,1,128]{2,1,0:T(1,128)S(1)}, u32[]{:S(2)}) copy-start(f32[4,1,128]{2,1,0:T(1,128)S(1)} %convert_element_type.305) | copy-start | bytes 6148
  21.1 13.4 %copy-start.4 = (bf16[1,1,512,512]{2,3,1,0:T(8,128)(2,1)}, bf16[1,1,512,512]{2,3,1,0:T(8,128)(2,1)S(1)}, u32[]{:S(2)}) copy-start(bf16[1,1,512,512]{2,3,1,0:T(8,128)(2,1)S(1)} %copy.203) | copy-start | bytes 1572868
  21.2 13.3 %copy-start.61 = (f32[512]{0:T(512)}, f32[512]{0:T(512)S(1)}, u32[]{:S(2)}) copy-start(f32[512]{0:T(512)S(1)} %broadcast_multiply_fusion.1) | copy-start | bytes 6148
  21.4 15.4 %copy-start.71 = (f32[512]{0:T(512)}, f32[512]{0:T(512)S(1)}, u32[]{:S(2)}) copy-start(f32[512]{0:T(512)S(1)} %fusion.176) | copy-start | bytes 6148
  21.4 15.3 %copy-start.67 = (f32[512]{0:T(512)}, f32[512]{0:T(512)S(1)}, u32[]{:S(2)}) copy-start(f32[512]{0:T(512)S(1)} %fusion.203) | copy-start | bytes 6148
  36.8 251.0 %all-gather.17.cloned.1.call-start = ((), (), s32[]{:S(2)}) async-start(), calls=%async_computation.7 | async-start | bytes 9437184 | tf_op jit(solution)/shard_map/all_gather | solution.py:175
  37.1 441.5 %copy-start.7 = (bf16[1,1,512,512]{2,3,1,0:T(8,128)(2,1)}, bf16[1,1,512,512]{2,3,1,0:T(8,128)(2,1)S(1)}, u32[]{:S(2)}) copy-start(bf16[1,1,512,512]{2,3,1,0:T(8,128)(2,1)S(1)} %copy.202) | copy-start | bytes 1572868
  40.9 440.4 %all-gather.19.cloned.1.call-start = ((), (), s32[]{:S(2)}) async-start(), calls=%async_computation.8 | async-start | bytes 2621440 | tf_op jit(solution)/shard_map/all_gather | solution.py:136
  41.5 444.9 %all-gather.21.cloned.1.call-start = ((), (), s32[]{:S(2)}) async-start(), calls=%async_computation.9 | async-start | bytes 2621440 | tf_op jit(solution)/shard_map/all_gather | solution.py:137
  42.1 788.4 %reduce-scatter.7.cloned.1.call-start = ((), (), s32[]{:S(2)}) async-start(), calls=%async_computation.11 | async-start | bytes 9437184 | tf_op jit(solution)/shard_map/reduce_scatter | solution.py:263
  138.6 23.2 %copy-start.92 = (bf16[128]{0:T(256)(128)(2,1)S(1)}, bf16[128]{0:T(256)(128)(2,1)}, u32[]{:S(2)}) copy-start(bf16[128]{0:T(256)(128)(2,1)} %param.37) | copy-start | bytes 772
  138.6 28.4 %copy-start.93 = (bf16[128]{0:T(256)(128)(2,1)S(1)}, bf16[128]{0:T(256)(128)(2,1)}, u32[]{:S(2)}) copy-start(bf16[128]{0:T(256)(128)(2,1)} %param.38) | copy-start | bytes 772
  138.6 33.4 %copy-start.94 = (bf16[128]{0:T(256)(128)(2,1)S(1)}, bf16[128]{0:T(256)(128)(2,1)}, u32[]{:S(2)}) copy-start(bf16[128]{0:T(256)(128)(2,1)} %param.39) | copy-start | bytes 772
  138.6 38.4 %copy-start.91 = (bf16[512]{0:T(512)(128)(2,1)S(1)}, bf16[512]{0:T(512)(128)(2,1)}, u32[]{:S(2)}) copy-start(bf16[512]{0:T(512)(128)(2,1)} %param.40) | copy-start | bytes 3076
  138.6 43.7 %copy-start.51 = (bf16[128,512]{1,0:T(8,128)(2,1)S(1)}, bf16[128,512]{1,0:T(8,128)(2,1)}, u32[]{:S(2)}) copy-start(bf16[128,512]{1,0:T(8,128)(2,1)} %param.32) | copy-start | bytes 393220
  138.6 50.9 %copy-start.28 = (bf16[2,1,512,512]{3,2,1,0:T(8,128)(2,1)S(1)}, bf16[2,1,512,512]{3,2,1,0:T(8,128)(2,1)}, u32[]{:S(2)}) copy-start(bf16[2,1,512,512]{3,2,1,0:T(8,128)(2,1)} %param.28) | copy-start | bytes 3145732
  161.7 33.0 %slice-start = ((bf16[512,1536]{1,0:T(8,128)(2,1)}), bf16[512,512]{1,0:T(8,128)(2,1)S(1)}, s32[]{:S(2)}) async-start(bf16[512,1536]{1,0:T(8,128)(2,1)} %copy-done.37), calls=%async_computation.18 | async-start | bytes 1048576 | tf_op jit(solution)/shard_map/slice | solution.py:173
  167.0 349.0 %copy-start.47 = (f32[4,1,128]{2,1,0:T(1,128)}, f32[4,1,128]{2,1,0:T(1,128)S(1)}, u32[]{:S(2)}) copy-start(f32[4,1,128]{2,1,0:T(1,128)S(1)} %convert_element_type.307) | copy-start | bytes 6148
  172.0 325.7 %copy-start.53 = (f32[4,1,128]{2,1,0:T(1,128)}, f32[4,1,128]{2,1,0:T(1,128)S(1)}, u32[]{:S(2)}) copy-start(f32[4,1,128]{2,1,0:T(1,128)S(1)} %convert_element_type.308) | copy-start | bytes 6148
  189.5 289.0 %copy-start.9 = (bf16[512,512]{1,0:T(8,128)(2,1)}, bf16[512,512]{1,0:T(8,128)(2,1)S(1)}, u32[]{:S(2)}) copy-start(bf16[512,512]{1,0:T(8,128)(2,1)S(1)} %all_gather.50) | copy-start | bytes 1572868
  371.0 6.3 copy-start.34
  424.7 5.7 copy-start.31
  479.1 36.9 %copy-start.2 = (f32[512,512]{0,1:T(8,128)}, f32[512,512]{0,1:T(8,128)S(1)}, u32[]{:S(2)}) copy-start(f32[512,512]{0,1:T(8,128)S(1)} %get-tuple-element.1175) | copy-start | bytes 3145732
  479.1 36.9 %copy-start.57 = (f32[512]{0:T(512)}, f32[512]{0:T(512)S(1)}, u32[]{:S(2)}) copy-start(f32[512]{0:T(512)S(1)} %broadcast_multiply_fusion.2) | copy-start | bytes 6148
  481.0 35.0 %copy-start = (f32[512,512]{0,1:T(8,128)}, f32[512,512]{0,1:T(8,128)S(1)}, u32[]{:S(2)}) copy-start(f32[512,512]{0,1:T(8,128)S(1)} %get-tuple-element.1177) | copy-start | bytes 3145732
  481.1 35.0 %copy-start.49 = (f32[512]{0:T(512)}, f32[512]{0:T(512)S(1)}, u32[]{:S(2)}) copy-start(f32[512]{0:T(512)S(1)} %broadcast_multiply_fusion) | copy-start | bytes 6148
  481.3 34.8 %copy-start.55 = (f32[512]{0:T(512)}, f32[512]{0:T(512)S(1)}, u32[]{:S(2)}) copy-start(f32[512]{0:T(512)S(1)} %get-tuple-element.1196) | copy-start | bytes 6148
  481.3 34.8 %copy-start.65 = (f32[512]{0:T(512)}, f32[512]{0:T(512)S(1)}, u32[]{:S(2)}) copy-start(f32[512]{0:T(512)S(1)} %get-tuple-element.1195) | copy-start | bytes 6148
  486.4 5.9 copy-start.38
  497.7 6.1 copy-start.29
  497.7 6.1 copy-start.96
  664.4 299.4 %reduce-scatter.9.cloned.1.call-start = ((), (), s32[]{:S(2)}) async-start(), calls=%async_computation.12 | async-start | bytes 9437184 | tf_op jit(solution)/shard_map/reduce_scatter | solution.py:263
  800.3 186.7 %reduce-scatter.13.cloned.1.call-start = ((), (), s32[]{:S(2)}) async-start(), calls=%async_computation.14 | async-start | bytes 655360 | tf_op jit(solution)/shard_map/reduce_scatter | solution.py:286
  803.2 218.0 %reduce-scatter.15.cloned.1.call-start = ((), (), s32[]{:S(2)}) async-start(), calls=%async_computation.15 | async-start | bytes 2621440 | tf_op jit(solution)/shard_map/reduce_scatter | solution.py:289
  809.2 245.8 %reduce-scatter.17.cloned.1.call-start = ((), (), s32[]{:S(2)}) async-start(), calls=%async_computation.16 | async-start | bytes 2621440 | tf_op jit(solution)/shard_map/reduce_scatter | solution.py:292
  815.1 271.4 %reduce-scatter.11.cloned.1.call-start = ((), (), s32[]{:S(2)}) async-start(), calls=%async_computation.13 | async-start | bytes 1966080 | tf_op jit(solution)/shard_map/reduce_scatter | solution.py:283
  830.5 133.3 %copy-start.6 = (bf16[1,1,512,512]{2,3,1,0:T(8,128)(2,1)S(1)}, bf16[1,1,512,512]{2,3,1,0:T(8,128)(2,1)}, u32[]{:S(2)}) copy-start(bf16[1,1,512,512]{2,3,1,0:T(8,128)(2,1)} %copy-done.4) | copy-start | bytes 1572868
  830.5 133.3 %copy-start.62 = (f32[512]{0:T(512)S(1)}, f32[512]{0:T(512)}, u32[]{:S(2)}) copy-start(f32[512]{0:T(512)} %copy-done.61) | copy-start | bytes 6148
  830.5 133.3 %copy-start.68 = (f32[512]{0:T(512)S(1)}, f32[512]{0:T(512)}, u32[]{:S(2)}) copy-start(f32[512]{0:T(512)} %copy-done.67) | copy-start | bytes 6148
  968.2 212.2 %all-reduce.12.cloned.1.call-start = ((), (), s32[]{:S(2)}) async-start(), calls=%async_computation.17 | async-start | bytes 3145728 | tf_op jit(solution)/shard_map/psum | solution.py:318
  977.6 6.8 copy-start.74
  981.3 105.2 %copy-start.27 = (bf16[1,1,512,512]{2,3,1,0:T(8,128)(2,1)S(1)}, bf16[1,1,512,512]{2,3,1,0:T(8,128)(2,1)}, u32[]{:S(2)}) copy-start(bf16[1,1,512,512]{2,3,1,0:T(8,128)(2,1)} %copy.204) | copy-start | bytes 1572868
  981.3 105.2 %copy-start.78 = (f32[512]{0:T(512)S(1)}, f32[512]{0:T(512)}, u32[]{:S(2)}) copy-start(f32[512]{0:T(512)} %copy-done.77) | copy-start | bytes 6148
  986.3 103.6 %copy-start.23 = (bf16[1,1,512,512]{2,3,1,0:T(8,128)(2,1)S(1)}, bf16[1,1,512,512]{2,3,1,0:T(8,128)(2,1)}, u32[]{:S(2)}) copy-start(bf16[1,1,512,512]{2,3,1,0:T(8,128)(2,1)} %copy.205) | copy-start | bytes 1572868
  986.3 103.6 %copy-start.76 = (f32[512]{0:T(512)S(1)}, f32[512]{0:T(512)}, u32[]{:S(2)}) copy-start(f32[512]{0:T(512)} %copy-done.75) | copy-start | bytes 6148
  (64 other events, 182.4 us)
Sparse Core Ops, SparseCore 0:
  9.6 22.3 all-gather.14
  36.9 125.5 all-gather.22
  164.7 123.0 all-gather.16
  289.2 20.7 all-gather.18
  311.5 22.5 all-gather.20
  664.5 147.1 reduce-scatter.6
  815.8 147.9 reduce-scatter.8
  966.3 20.6 reduce-scatter.12
  989.7 31.4 reduce-scatter.14
  1023.5 31.4 reduce-scatter.16
  1058.3 28.1 reduce-scatter.10
  1090.2 90.2 all-reduce.11
where the time goes:
time: 1210 us; the launch traced here: 1200 us
  matrix products  395 us (33%)
  waiting for transfers between devices  301 us (25%)
  local copies, waits for them, and re-layouts  193 us (16%)
  other arithmetic  155 us (13%)
  blocking collectives  131 us (11%)
  between operations  17.2 us (1%)
    reduce_scatter x2, waiting for transfers between devices, body(): lax.psum_scatter(kv_terms.reshape(seq_len, 2 * model_width).astype(jnp.bf...  129 us
    dot_general x32, matrix products, score_block(): jnp.einsum('qhd,khd->hqk', query_heads, key_heads, preferred_element_type...  77.9 us
    dot_general x16, matrix products, attend_visit(): jnp.einsum('hqk,khd->qhd', soft_low, value_heads, preferred_element_type=...  66.4 us
    dot_general x16, matrix products, grad_block(): jnp.einsum('qhd,khd->hqk', grad_heads, value_heads, preferred_element_typ...  64.5 us
    mul x48, other arithmetic, body(): own_pos = own_blocks[row_ids // BLK] * BLK + row_ids % BLK  62.6 us
    unnamed x219, local copies, waits for them, and re-layouts  55.3 us
    all_gather x2, blocking collectives, body(): lax.all_gather(segment_ids[micro_idx, 0], 'ctx', axis=0, tiled=True)  53.6 us
    dot_general x16, matrix products, grad_block(): jnp.einsum('hqk,khd->qhd', grad_scores, key_heads, preferred_element_type...  50 us
  transfers between devices with their start and end apart: 12, of which 8 were waited for; matrix products, arithmetic and copies ran while one was open for 46% of the time, Pallas kernels for 0%

commit v1 on v0

--- a/solution.py
+++ b/solution.py
@@ -3,12 +3,18 @@
 import jax.numpy as jnp
 from jax import lax
 from jax.sharding import PartitionSpec as P
+from jax.lax import all_gather
 
 H = 8
 HD = 64
 BLK = 256
 norm_eps = 1e-05
 mask_fill = -1e30
+
+
+def link_types(vec):
+    b_now = jnp.sum(all_gather(vec, "ctx"), 0)
+    return b_now
 
 
 def layer_norm(values, gain_vec, offset):
@@ -315,7 +321,7 @@
         ).astype(jnp.float32),
     )
     summed = (
-        lax.psum(owned[0].astype(jnp.bfloat16), "ctx").astype(jnp.float32),
+        link_types(owned[0].astype(jnp.bfloat16)).astype(jnp.float32),
         lax.psum(owned[1].astype(jnp.bfloat16), "ctx").astype(jnp.float32),
         lax.psum(owned[2].astype(jnp.bfloat16), "ctx").astype(jnp.float32),
         lax.psum(owned[3].astype(jnp.bfloat16), "ctx").astype(jnp.float32),

time: 1210 us -> 1260 us (1.041)
  waiting for transfers between devices: 301 us -> 354 us
    psum x1, waiting for transfers between devices: 48.7 us -> 70.8 us  [body(): lax.psum(owned[1].astype(jnp.bfloat16), 'ctx').astype(jnp.float32)]
    reduce_scatter x1, waiting for transfers between devices: 0.6 us -> 19.1 us  [body(): lax.psum_scatter(grad_sums[1].astype(jnp.bfloat16), 'fsdp', scatter_dimen...]
    unnamed x219 -> x225, local copies, waits for them, and re-layouts: 55.3 us -> 55.7 us
  transfers between devices with their start and end apart: 12 -> 13, of which waited for: 8 -> 9; matrix products, arithmetic and copies ran while one was open for 46% -> 44% of each run, Pallas kernels for 0% -> 0%
where the time goes in v1:
time: 1260 us; the launch traced here: 1240 us
  matrix products  393 us (31%)
  waiting for transfers between devices  354 us (28%)
  local copies, waits for them, and re-layouts  195 us (15%)
  other arithmetic  153 us (12%)
  blocking collectives  129 us (10%)
  between operations  16.9 us (1%)
    reduce_scatter x2, waiting for transfers between devices, body(): lax.psum_scatter(kv_terms.reshape(seq_len, 2 * model_width).astype(jnp.bf...  138 us
    dot_general x32, matrix products, score_block(): jnp.einsum('qhd,khd->hqk', query_heads, key_heads, preferred_element_type...  77.9 us
    psum x1, waiting for transfers between devices, body(): lax.psum(owned[1].astype(jnp.bfloat16), 'ctx').astype(jnp.float32)  70.8 us
    dot_general x16, matrix products, attend_visit(): jnp.einsum('hqk,khd->qhd', soft_low, value_heads, preferred_element_type=...  66.4 us
    dot_general x16, matrix products, grad_block(): jnp.einsum('qhd,khd->hqk', grad_heads, value_heads, preferred_element_typ...  64.4 us
    mul x48, other arithmetic, body(): own_pos = own_blocks[row_ids // BLK] * BLK + row_ids % BLK  62.6 us
    unnamed x225, local copies, waits for them, and re-layouts  55.7 us
    all_gather x2, blocking collectives, body(): lax.all_gather(segment_ids[micro_idx, 0], 'ctx', axis=0, tiled=True)  53.5 us
  transfers between devices with their start and end apart: 13, of which 9 were waited for; matrix products, arithmetic and copies ran while one was open for 44% of the time, Pallas kernels for 0%

profile of v1, /device:TPU:0, one launch (start us, length us, event | category | flops | bytes accessed | tf_op | source)
XLA Modules:
  0.0 1244.4 jit_solution(16536931727020067586)
XLA Ops:
  8.0 6.2 all-gather.3
  14.1 5.4 all-gather.4
  21.4 10.5 all-gather.17.cloned.1.call-done
  45.4 27.0 %all-gather = s32[1,1,4096]{2,1,0:T(1,128)S(1)} all-gather(s32[1,1,512]{2,1,0:T(1,128)S(1)} %get-tuple-element.1147), channel_id=2, replica_groups=mesh['ctx'=8,'fsdp'=4] {'ctx'}, dimensions={2}, use_global_device_ids=true | all-gather | bytes 18432 | tf_op jit(solution)/shard_map/all_gather | solution.py:182
  72.4 4.2 compare_select_fusion.14
  76.6 5.8 select_multiply_fusion.2
  85.7 23.0 %gather_fusion.1 = s32[4096]{0:T(1024)S(1)} fusion(s32[4096]{0:T(1024)S(1)} %bitcast.528, s32[4096]{0:T(1024)S(1)} %broadcast_clamp_fusion), kind=kCustom, calls=%fused_computation.1 | custom fusion | bytes 49152 | tf_op jit(solution)/shard_map/gather | solution.py:184
  108.7 26.5 %all-gather.1 = s32[1,1,4096]{2,1,0:T(1,128)S(1)} all-gather(s32[1,1,512]{2,1,0:T(1,128)S(1)} %get-tuple-element.1148), channel_id=3, replica_groups=mesh['ctx'=8,'fsdp'=4] {'ctx'}, dimensions={2}, use_global_device_ids=true | all-gather | bytes 18432 | tf_op jit(solution)/shard_map/all_gather | solution.py:182
  138.4 23.0 %gather_fusion.3 = s32[4096]{0:T(1024)S(1)} fusion(s32[4096]{0:T(1024)S(1)} %bitcast.530, s32[4096]{0:T(1024)S(1)} %broadcast_clamp_fusion), kind=kCustom, calls=%fused_computation.3 | custom fusion | bytes 49152 | tf_op jit(solution)/shard_map/gather | solution.py:184
  161.6 5.2 all-gather.6
  166.7 5.0 all-gather.7
  171.8 5.0 all-gather.5
  176.8 5.2 all-gather.8
  182.1 7.2 all_gather.56
  194.9 11.6 copy.162
  206.5 12.2 copy.239
  218.7 5.3 slice_bitcast_fusion
  227.4 50.1 %while.76 = (s32[]{:T(128)}, f32[8,512]{1,0:T(8,128)S(1)}, f32[8,512]{1,0:T(8,128)S(1)}, s32[512]{0:T(512)S(1)}, s32[8,512]{1,0:T(8,128)S(1)}, /*index=5*/s32[8,...) while((s32[]{:T(128)}, f32[8,512]{1,0:T(8,128)S(1)}, ...), condition=%wide.region_15.16_spmd.clone, body=%wide.region_12.15_spmd.clone.sunk | while | flops 286030336 | bytes 18847896 | solution.py:60
  277.5 10.3 all-gather.19.cloned.1.call-done
  287.8 12.0 copy.155
  299.9 12.3 copy.238
  312.1 5.3 slice_bitcast_fusion.2
  320.8 50.5 %while.74 = (s32[]{:T(128)}, f32[8,512]{1,0:T(8,128)S(1)}, f32[8,512]{1,0:T(8,128)S(1)}, s32[512]{0:T(512)S(1)}, s32[8,512]{1,0:T(8,128)S(1)}, /*index=5*/s32[8,...) while((s32[]{:T(128)}, f32[8,512]{1,0:T(8,128)S(1)}, ...), condition=%wide.region_5.6_spmd.clone, body=%wide.region_2.5_spmd.clone.sunk | while | flops 286030336 | bytes 18847896 | solution.py:60
  371.3 5.7 copy.158
  377.6 46.4 %while.75 = (s32[]{:T(128)}, f32[512,8,64]{0,2,1:T(8,128)S(1)}, bf16[8,512,8,64]{1,3,2,0:T(8,128)(2,1)}, s32[512]{0:T(512)S(1)}, s32[8,512]{1,0:T(8,128)S(1)}, /...) while((s32[]{:T(128)}, f32[512,8,64]{0,2,1:T(8,128)S(1)}, ...), condition=%wide.region_7.8_spmd.clone, body=%wide.region_6.7_spmd.clone.sunk | while | flops 546580992 | bytes 4234906 | solution.py:81
  379.3 4.2 fusion.351
  402.5 4.2 fusion.351
  425.0 5.7 copy.165
  430.7 46.4 %while.77 = (s32[]{:T(128)}, f32[512,8,64]{0,2,1:T(8,128)S(1)}, bf16[8,512,8,64]{1,3,2,0:T(8,128)(2,1)}, s32[512]{0:T(512)S(1)}, s32[8,512]{1,0:T(8,128)S(1)}, /...) while((s32[]{:T(128)}, f32[512,8,64]{0,2,1:T(8,128)S(1)}, ...), condition=%wide.region_17.18_spmd.clone, body=%wide.region_16.17_spmd.clone.sunk | while | flops 546580992 | bytes 4234906 | solution.py:81
  481.7 5.1 fusion.219
  486.8 5.9 convert_reduce_fusion
  498.1 6.1 multiply_convert_fusion.1
  521.5 4.3 broadcast.709.clone2
  525.8 139.2 %while.78 = (s32[]{:T(128)}, f32[512,8,64]{0,2,1:T(8,128)}, bf16[8,512,1024]{2,1,0:T(8,128)(2,1)}, bf16[8,512,8,64]{1,3,2,0:T(8,128)(2,1)}, s32[512]{0:T(512)S(1...) while((s32[]{:T(128)}, f32[512,8,64]{0,2,1:T(8,128)}, ...), condition=%wide.region_24.25_spmd.clone, body=%wide.region_23.24_spmd.clone.sunk | while | flops 1367353856 | bytes 51714240 | solution.py:264
  665.1 4.3 broadcast.709.clone2.1
  669.4 131.5 %while.79 = (s32[]{:T(128)}, f32[512,8,64]{0,2,1:T(8,128)}, bf16[8,512,1024]{2,1,0:T(8,128)(2,1)}, bf16[8,512,8,64]{1,3,2,0:T(8,128)(2,1)}, s32[512]{0:T(512)S(1...) while((s32[]{:T(128)}, f32[512,8,64]{0,2,1:T(8,128)}, ...), condition=%wide.region_32.33_spmd.clone, body=%wide.region_31.32_spmd.clone.sunk | while | flops 1367353856 | bytes 51714240 | solution.py:264
  822.6 4.2 fusion.179
  826.8 137.7 %reduce-scatter.9.cloned.1.call-done = bf16[512,1024]{1,0:T(8,128)(2,1)} async-done(((bf16[4096,1024]{1,0:T(8,128)(2,1)}), bf16[512,1024]{1,0:T(8,128)(2,1)}) %reduce-scatter.9.cloned.1.call-update) | async-done | bytes 1048592 | tf_op jit(solution)/shard_map/reduce_scatter | solution.py:269
  964.5 4.6 fusion.144
  969.2 19.1 %reduce-scatter.13.cloned.1.call-done = bf16[128,512]{1,0:T(8,128)(2,1)} async-done(((bf16[512,512]{1,0:T(8,128)(2,1)}), bf16[128,512]{1,0:T(8,128)(2,1)}) %reduce-scatter.13.cloned.1.call-update) | async-done | bytes 131088 | tf_op jit(solution)/shard_map/reduce_scatter | solution.py:292
  988.2 34.2 %reduce-scatter.15.cloned.1.call-done = bf16[128,2048]{1,0:T(8,128)(2,1)} async-done(((bf16[512,2048]{1,0:T(8,128)(2,1)}), bf16[128,2048]{1,0:T(8,128)(2,1)}) %reduce-scatter.15.cloned.1.call-update) | async-done | bytes 524304 | tf_op jit(solution)/shard_map/reduce_scatter | solution.py:295
  1022.4 33.9 %reduce-scatter.17.cloned.1.call-done = bf16[512,512]{1,0:T(8,128)(2,1)} async-done(((bf16[2048,512]{1,0:T(8,128)(2,1)}), bf16[512,512]{1,0:T(8,128)(2,1)}) %reduce-scatter.17.cloned.1.call-update) | async-done | bytes 524304 | tf_op jit(solution)/shard_map/reduce_scatter | solution.py:298
  1056.3 30.8 %reduce-scatter.11.cloned.1.call-done = bf16[128,1536]{1,0:T(8,128)(2,1)} async-done(((bf16[512,1536]{1,0:T(8,128)(2,1)}), bf16[128,1536]{1,0:T(8,128)(2,1)}) %reduce-scatter.11.cloned.1.call-update) | async-done | bytes 393232 | tf_op jit(solution)/shard_map/reduce_scatter | solution.py:289
  1089.1 5.0 all-gather.9
  1100.9 70.8 %all-reduce.12.cloned.1.call-done = (bf16[128,512]{1,0:T(8,128)(2,1)}, bf16[128,2048]{1,0:T(8,128)(2,1)}, bf16[512,512]{1,0:T(8,128)(2,1)}) async-done(((bf16[128,512]{1,0:T(8,128)(2,1)}, bf16[128,2048]{1,0:T(8,128)(2,1)}, bf16[512,512]{1,0:T(8,128)(2,1)}), (bf16[128,512]{1,0:T(8,128)(2,1)}, bf16[128,2048]{1,0:T(8,128)(2,1)}, bf16[512,512]{1,0:T(8,128)(2,1)})) %all-reduce.12.cloned.1.call-update) | async-done | bytes 1179664 | tf_op jit(solution)/shard_map/psum | solution.py:325
  1191.0 11.3 all-reduce.9
  1202.8 19.7 %all-reduce.7 = (bf16[128]{0:T(256)(128)(2,1)S(1)}, bf16[128]{0:T(256)(128)(2,1)S(1)}, bf16[128]{0:T(256)(128)(2,1)S(1)}, bf16[128]{0:T(256)(128)(2,1)S(1)}, bf1...) all-reduce(bf16[128]{0:T(256)(128)(2,1)S(1)} %dynamic-slice.1, ...), channel_id=1, replica_groups=mesh['ctx'=8,'fsdp'=4] {'ctx'}, use_global_device_ids=true, to_apply=%region_47.48 | all-reduce | flops 1280 | bytes 5120 | tf_op jit(solution)/shard_map/psum | solution.py:328
  1229.7 4.5 all-gather.27.cloned.1.call-done
  (793 shorter events, 574.1 us)
Async XLA Ops:
  7.2 24.8 %all-gather.17.cloned.1.call-start = ((), (), s32[]{:S(2)}) async-start(), calls=%async_computation.6 | async-start | bytes 1966080 | tf_op jit(solution)/shard_map/all_gather | solution.py:140
  7.9 187.0 %all-gather.25.cloned.1.call-start = ((), (), s32[]{:S(2)}) async-start(), calls=%async_computation.10 | async-start | bytes 9437184 | tf_op jit(solution)/shard_map/all_gather | solution.py:181
  14.1 23.3 %copy-start.61 = (f32[4,1,128]{2,1,0:T(1,128)}, f32[4,1,128]{2,1,0:T(1,128)S(1)}, u32[]{:S(2)}) copy-start(f32[4,1,128]{2,1,0:T(1,128)S(1)} %convert_element_type.306) | copy-start | bytes 6148
  19.5 17.9 %copy-start.89 = (f32[4,1,128]{2,1,0:T(1,128)}, f32[4,1,128]{2,1,0:T(1,128)S(1)}, u32[]{:S(2)}) copy-start(f32[4,1,128]{2,1,0:T(1,128)S(1)} %convert_element_type.307) | copy-start | bytes 6148
  21.1 13.4 %copy-start.4 = (bf16[1,1,512,512]{2,3,1,0:T(8,128)(2,1)}, bf16[1,1,512,512]{2,3,1,0:T(8,128)(2,1)S(1)}, u32[]{:S(2)}) copy-start(bf16[1,1,512,512]{2,3,1,0:T(8,128)(2,1)S(1)} %copy.203) | copy-start | bytes 1572868
  21.2 13.3 %copy-start.63 = (f32[512]{0:T(512)}, f32[512]{0:T(512)S(1)}, u32[]{:S(2)}) copy-start(f32[512]{0:T(512)S(1)} %broadcast_multiply_fusion.1) | copy-start | bytes 6148
  21.4 15.4 %copy-start.73 = (f32[512]{0:T(512)}, f32[512]{0:T(512)S(1)}, u32[]{:S(2)}) copy-start(f32[512]{0:T(512)S(1)} %fusion.176) | copy-start | bytes 6148
  21.4 15.3 %copy-start.69 = (f32[512]{0:T(512)}, f32[512]{0:T(512)S(1)}, u32[]{:S(2)}) copy-start(f32[512]{0:T(512)S(1)} %fusion.203) | copy-start | bytes 6148
  36.8 251.0 %all-gather.19.cloned.1.call-start = ((), (), s32[]{:S(2)}) async-start(), calls=%async_computation.7 | async-start | bytes 9437184 | tf_op jit(solution)/shard_map/all_gather | solution.py:181
  37.1 441.9 %copy-start.7 = (bf16[1,1,512,512]{2,3,1,0:T(8,128)(2,1)}, bf16[1,1,512,512]{2,3,1,0:T(8,128)(2,1)S(1)}, u32[]{:S(2)}) copy-start(bf16[1,1,512,512]{2,3,1,0:T(8,128)(2,1)S(1)} %copy.202) | copy-start | bytes 1572868
  40.9 440.8 %all-gather.21.cloned.1.call-start = ((), (), s32[]{:S(2)}) async-start(), calls=%async_computation.8 | async-start | bytes 2621440 | tf_op jit(solution)/shard_map/all_gather | solution.py:142
  41.5 445.3 %all-gather.23.cloned.1.call-start = ((), (), s32[]{:S(2)}) async-start(), calls=%async_computation.9 | async-start | bytes 2621440 | tf_op jit(solution)/shard_map/all_gather | solution.py:143
  42.0 780.5 %reduce-scatter.7.cloned.1.call-start = ((), (), s32[]{:S(2)}) async-start(), calls=%async_computation.11 | async-start | bytes 9437184 | tf_op jit(solution)/shard_map/reduce_scatter | solution.py:269
  138.3 23.2 %copy-start.94 = (bf16[128]{0:T(256)(128)(2,1)S(1)}, bf16[128]{0:T(256)(128)(2,1)}, u32[]{:S(2)}) copy-start(bf16[128]{0:T(256)(128)(2,1)} %param.37) | copy-start | bytes 772
  138.4 28.4 %copy-start.95 = (bf16[128]{0:T(256)(128)(2,1)S(1)}, bf16[128]{0:T(256)(128)(2,1)}, u32[]{:S(2)}) copy-start(bf16[128]{0:T(256)(128)(2,1)} %param.38) | copy-start | bytes 772
  138.4 33.4 %copy-start.96 = (bf16[128]{0:T(256)(128)(2,1)S(1)}, bf16[128]{0:T(256)(128)(2,1)}, u32[]{:S(2)}) copy-start(bf16[128]{0:T(256)(128)(2,1)} %param.39) | copy-start | bytes 772
  138.4 38.4 %copy-start.93 = (bf16[512]{0:T(512)(128)(2,1)S(1)}, bf16[512]{0:T(512)(128)(2,1)}, u32[]{:S(2)}) copy-start(bf16[512]{0:T(512)(128)(2,1)} %param.40) | copy-start | bytes 3076
  138.4 43.7 %copy-start.53 = (bf16[128,512]{1,0:T(8,128)(2,1)S(1)}, bf16[128,512]{1,0:T(8,128)(2,1)}, u32[]{:S(2)}) copy-start(bf16[128,512]{1,0:T(8,128)(2,1)} %param.32) | copy-start | bytes 393220
  138.4 50.9 %copy-start.31 = (bf16[2,1,512,512]{3,2,1,0:T(8,128)(2,1)S(1)}, bf16[2,1,512,512]{3,2,1,0:T(8,128)(2,1)}, u32[]{:S(2)}) copy-start(bf16[2,1,512,512]{3,2,1,0:T(8,128)(2,1)} %param.28) | copy-start | bytes 3145732
  161.5 33.0 %slice-start = ((bf16[512,1536]{1,0:T(8,128)(2,1)}), bf16[512,512]{1,0:T(8,128)(2,1)S(1)}, s32[]{:S(2)}) async-start(bf16[512,1536]{1,0:T(8,128)(2,1)} %copy-done.40), calls=%async_computation.19 | async-start | bytes 1048576 | tf_op jit(solution)/shard_map/slice | solution.py:179
  166.7 349.6 %copy-start.49 = (f32[4,1,128]{2,1,0:T(1,128)}, f32[4,1,128]{2,1,0:T(1,128)S(1)}, u32[]{:S(2)}) copy-start(f32[4,1,128]{2,1,0:T(1,128)S(1)} %convert_element_type.309) | copy-start | bytes 6148
  171.8 326.3 %copy-start.55 = (f32[4,1,128]{2,1,0:T(1,128)}, f32[4,1,128]{2,1,0:T(1,128)S(1)}, u32[]{:S(2)}) copy-start(f32[4,1,128]{2,1,0:T(1,128)S(1)} %convert_element_type.310) | copy-start | bytes 6148
  189.3 289.6 %copy-start.9 = (bf16[512,512]{1,0:T(8,128)(2,1)}, bf16[512,512]{1,0:T(8,128)(2,1)S(1)}, u32[]{:S(2)}) copy-start(bf16[512,512]{1,0:T(8,128)(2,1)S(1)} %all_gather.56) | copy-start | bytes 1572868
  371.3 6.3 copy-start.37
  479.5 36.9 %copy-start.2 = (f32[512,512]{0,1:T(8,128)}, f32[512,512]{0,1:T(8,128)S(1)}, u32[]{:S(2)}) copy-start(f32[512,512]{0,1:T(8,128)S(1)} %get-tuple-element.1174) | copy-start | bytes 3145732
  479.5 36.9 %copy-start.59 = (f32[512]{0:T(512)}, f32[512]{0:T(512)S(1)}, u32[]{:S(2)}) copy-start(f32[512]{0:T(512)S(1)} %broadcast_multiply_fusion.2) | copy-start | bytes 6148
  481.4 35.0 %copy-start = (f32[512,512]{0,1:T(8,128)}, f32[512,512]{0,1:T(8,128)S(1)}, u32[]{:S(2)}) copy-start(f32[512,512]{0,1:T(8,128)S(1)} %get-tuple-element.1176) | copy-start | bytes 3145732
  481.4 35.0 %copy-start.51 = (f32[512]{0:T(512)}, f32[512]{0:T(512)S(1)}, u32[]{:S(2)}) copy-start(f32[512]{0:T(512)S(1)} %broadcast_multiply_fusion) | copy-start | bytes 6148
  481.6 34.8 %copy-start.57 = (f32[512]{0:T(512)}, f32[512]{0:T(512)S(1)}, u32[]{:S(2)}) copy-start(f32[512]{0:T(512)S(1)} %get-tuple-element.1195) | copy-start | bytes 6148
  481.6 34.8 %copy-start.67 = (f32[512]{0:T(512)}, f32[512]{0:T(512)S(1)}, u32[]{:S(2)}) copy-start(f32[512]{0:T(512)S(1)} %get-tuple-element.1194) | copy-start | bytes 6148
  665.0 299.5 %reduce-scatter.9.cloned.1.call-start = ((), (), s32[]{:S(2)}) async-start(), calls=%async_computation.12 | async-start | bytes 9437184 | tf_op jit(solution)/shard_map/reduce_scatter | solution.py:269
  801.1 187.2 %reduce-scatter.13.cloned.1.call-start = ((), (), s32[]{:S(2)}) async-start(), calls=%async_computation.14 | async-start | bytes 655360 | tf_op jit(solution)/shard_map/reduce_scatter | solution.py:292
  804.0 218.5 %reduce-scatter.15.cloned.1.call-start = ((), (), s32[]{:S(2)}) async-start(), calls=%async_computation.15 | async-start | bytes 2621440 | tf_op jit(solution)/shard_map/reduce_scatter | solution.py:295
  809.9 246.3 %reduce-scatter.17.cloned.1.call-start = ((), (), s32[]{:S(2)}) async-start(), calls=%async_computation.16 | async-start | bytes 2621440 | tf_op jit(solution)/shard_map/reduce_scatter | solution.py:298
  815.8 6.8 copy-start.8
  815.8 6.8 copy-start.62
  815.8 6.8 copy-start.66
  815.8 6.8 copy-start.72
  815.8 6.8 copy-start.90
  815.8 271.3 %reduce-scatter.11.cloned.1.call-start = ((), (), s32[]{:S(2)}) async-start(), calls=%async_computation.13 | async-start | bytes 1966080 | tf_op jit(solution)/shard_map/reduce_scatter | solution.py:289
  818.3 146.2 %copy-start.6 = (bf16[1,1,512,512]{2,3,1,0:T(8,128)(2,1)S(1)}, bf16[1,1,512,512]{2,3,1,0:T(8,128)(2,1)}, u32[]{:S(2)}) copy-start(bf16[1,1,512,512]{2,3,1,0:T(8,128)(2,1)} %copy-done.4) | copy-start | bytes 1572868
  818.3 146.2 %copy-start.64 = (f32[512]{0:T(512)S(1)}, f32[512]{0:T(512)}, u32[]{:S(2)}) copy-start(f32[512]{0:T(512)} %copy-done.63) | copy-start | bytes 6148
  818.3 146.2 %copy-start.70 = (f32[512]{0:T(512)S(1)}, f32[512]{0:T(512)}, u32[]{:S(2)}) copy-start(f32[512]{0:T(512)} %copy-done.69) | copy-start | bytes 6148
  826.8 260.4 %copy-start.101 = (u32[32]{0:T(128)S(1)}, u32[32]{0:T(128)}, u32[]{:S(2)}) copy-start(u32[32]{0:T(128)} %constant.231) | copy-start | bytes 388
  826.8 262.2 %copy-start.97 = (bf16[128]{0:T(256)(128)(2,1)S(1)}, bf16[128]{0:T(256)(128)(2,1)}, u32[]{:S(2)}) copy-start(bf16[128]{0:T(256)(128)(2,1)} %param.41) | copy-start | bytes 772
  969.1 202.5 %all-reduce.12.cloned.1.call-start = ((), (), s32[]{:S(2)}) async-start(), calls=%async_computation.18 | async-start | bytes 2359296 | tf_op jit(solution)/shard_map/psum | solution.py:325
  1056.3 178.0 %all-gather.27.cloned.1.call-start = ((), (), s32[]{:S(2)}) async-start(), calls=%async_computation.17 | async-start | bytes 3538944 | tf_op jit(solution)/shard_map/all_gather | solution.py:16
  1099.3 78.2 %copy-start.48 = (bf16[512,512]{1,0:T(8,128)(2,1)S(1)}, bf16[512,512]{1,0:T(8,128)(2,1)}, u32[]{:S(2)}) copy-start(bf16[512,512]{1,0:T(8,128)(2,1)} %copy.173) | copy-start | bytes 1572868
  (68 other events, 195.9 us)
Sparse Core Ops, SparseCore 0:
  9.6 22.3 all-gather.16
  36.9 125.5 all-gather.24
  164.7 123.1 all-gather.18
  289.3 20.7 all-gather.20
  311.5 22.5 all-gather.22
  665.2 147.1 reduce-scatter.6
  816.4 148.0 reduce-scatter.8
  967.6 20.6 reduce-scatter.12
  990.9 31.4 reduce-scatter.14
  1024.8 31.4 reduce-scatter.16
  1059.0 28.1 reduce-scatter.10
  1090.8 80.7 all-reduce.11
  1174.1 60.1 all-gather.26
